TPU v7x, 32 devices: a whole 2x2x4 slice. The times are simulated.
32 devices in a mesh: parts: 2 (over y), lon: 4 (over z), lat: 2 (over core), chan: 2 (over x).
Axes of the slice: x: 2, y: 2, z: 4, core: 2. Of those that a mesh axis runs over, the one named last changes fastest.
Arguments:
- fine_act: bfloat16 [384, 896, 256], P(('parts', 'lat', 'chan'), 'lon'), parts along dimension 0, may hold values from -6 to 6
- coarse_grad: bfloat16 [192, 448, 128], P(('parts', 'lat'), 'lon', 'chan'), parts along dimension 0, may hold values from -6 to 6
- kernel: bfloat16 [3, 3, 256, 128], replicated, may hold values from -0.125 to 0.125
Outputs:
- input_grad: bfloat16 [384, 896, 256], P(('parts', 'lat', 'chan'), 'lon'), parts along dimension 0
- kernel_grad: float32 [6, 3, 256, 128], P('parts'), parts along dimension 0
There are 2 independent parts, one for each index of `parts`. A program takes and returns all parts, laid end to end along the dimension named above; an argument that names none is the same for every part. Nothing has to cross between parts.
All inputs are finite; a program needn't handle non-finite values.
Results may differ from a plain program's by a relative error of at most 0.001.
Values may be sent and summed in bfloat16 or wider, within the bound.
A program may use at most 64 MiB of HBM per device.

v0:
```python
import functools
import math

import jax
import jax.numpy as jnp
from jax import lax
from jax.experimental import pallas as pl
from jax.experimental.pallas import tpu as pltpu
from jax.sharding import PartitionSpec as P

MESH = pl.DeviceIdType.MESH
LANES = 128
F32 = jnp.float32
BF16 = jnp.bfloat16
TAP_ORDER = (1, 0, 2)
AXES = ("lon", "lat", "chan")


def one_hot(shape, test):
    rows = lax.broadcasted_iota(jnp.int32, shape, 0)
    cols = lax.broadcasted_iota(jnp.int32, shape, 1)
    return jnp.where(test(rows, cols), 1.0, 0.0).astype(BF16)


def share(rows, peers, unit):
    for size in range(unit, rows + 1, unit):
        if rows % size == 0 and rows // size <= peers:
            return size
    raise ValueError("no share")


def stage_plan(rows, order, sizes):
    plan = []
    for position, axis in enumerate(order):
        unit = 8
        for later in order[position + 1:]:
            unit *= sizes[later] if later != "lon" else 1
        part = share(rows, sizes[axis], unit)
        plan.append((axis, part, rows // part))
        rows = part
    return plan


def grads_kernel(
    sizes, half_rows, half_cols, out_ch, scale,
    fine, cg, kernel, rows_out, kg_out,
    fbuf, kcat, tiles, taps, even_t, edge_out, edge_in, spots, acc, rows_buf, row_sem, *rest,
):
    landing, (local_sem, tile_recv, tile_send, edge_send, edge_recv, red_send, red_recv, gat_send, gat_recv) = rest[:-9], rest[-9:]
    lon_n, lat_n, chan_n = (sizes[a] for a in AXES)
    me = {a: lax.axis_index(a) for a in AXES}
    lat, chan = me["lat"], me["chan"]
    h = half_rows
    group = group_size(h + 2)
    spans = [(max(1, q * group), min(h + 1, (q + 1) * group)) for q in range((h + 2) // group)]
    width = cg.shape[1]
    in_ch = fbuf.shape[2]
    mine = pl.ds(pl.multiple_of(chan * width, width), width)

    def other(axis, step):
        return lax.rem(me[axis] + step, sizes[axis])

    local = [pltpu.make_async_copy(fine.at[:, 0], fbuf, local_sem.at[0])]
    for r in range(3):
        for s in range(3):
            local.append(
                pltpu.make_async_copy(
                    kernel.at[r, s], kcat.at[r, :, pl.ds(s * out_ch, out_ch)], local_sem.at[1 + 3 * r + s]
                )
            )
    for copy in local:
        copy.start()

    is_top = jnp.logical_and(lat == 0, chan == 0)
    is_bottom = jnp.logical_and(lat == lat_n - 1, chan == chan_n - 1)
    for q, (lo, hi) in enumerate(spans):
        pltpu.make_async_copy(
            cg.at[pl.ds(chan * h + lo - 1, hi - lo)], tiles.at[pl.ds(lo, hi - lo), mine], tile_recv.at[2 + q]
        ).start()

    @pl.when(chan > 0)
    def _():
        pltpu.make_async_copy(cg.at[chan * h - 1], tiles.at[0, mine], tile_recv.at[0]).start()

    @pl.when(chan < chan_n - 1)
    def _():
        pltpu.make_async_copy(cg.at[(chan + 1) * h], tiles.at[h + 1, mine], tile_recv.at[1]).start()

    barrier = pltpu.get_barrier_semaphore()
    greeted = 0
    for dl in range(lat_n):
        for dc in range(chan_n):
            if dl or dc:
                pl.semaphore_signal(
                    barrier, inc=1, device_id={"lat": other("lat", dl), "chan": other("chan", dc)}, device_id_type=MESH
                )
                greeted += 1
    for d in range(1, lon_n):
        pl.semaphore_signal(barrier, inc=1, device_id={"lon": other("lon", d)}, device_id_type=MESH)
        greeted += 1
    pl.semaphore_wait(barrier, greeted)

    sends = []

    def send(condition, src, dst, send_sem, recv_sem, where):
        copy = pltpu.make_async_remote_copy(
            src_ref=src, dst_ref=dst, send_sem=send_sem, recv_sem=recv_sem, device_id=where, device_id_type=MESH
        )
        if condition is None:
            copy.start()
        else:
            pl.when(condition)(lambda: copy.start())
        sends.append((condition, copy))

    slot = 0
    for d in range(1, chan_n):
        p = other("chan", d)
        send(p > 0, cg.at[jnp.maximum(p * h - 1, 0)], tiles.at[0, mine], tile_send.at[slot], tile_recv.at[0], {"chan": p})
        slot += 1
    send(
        lat < lat_n - 1, cg.at[chan_n * h - 1], tiles.at[0, mine], tile_send.at[slot], tile_recv.at[0],
        {"lat": jnp.minimum(lat + 1, lat_n - 1), "chan": 0},
    )
    send(
        lat > 0, cg.at[0], tiles.at[h + 1, mine], tile_send.at[slot + 1], tile_recv.at[1],
        {"lat": jnp.maximum(lat - 1, 0), "chan": chan_n - 1},
    )
    slot += 2
    for q, (lo, hi) in enumerate(spans):
        for d in range(1, chan_n):
            p = other("chan", d)
            send(
                None, cg.at[pl.ds(p * h + lo - 1, hi - lo)], tiles.at[pl.ds(lo, hi - lo), mine],
                tile_send.at[slot], tile_recv.at[2 + q], {"chan": p},
            )
            slot += 1
    for d in range(1, chan_n):
        p = other("chan", d)
        send(
            p < chan_n - 1, cg.at[jnp.minimum((p + 1) * h, chan_n * h - 1)], tiles.at[h + 1, mine],
            tile_send.at[slot], tile_recv.at[1], {"chan": p},
        )
        slot += 1

    local[0].wait()
    pick = one_hot((2 * half_cols, LANES), lambda row, col: row == 2 * col)

    def take_even(i, _):
        picked = lax.dot_general(fbuf[i], pick, (((0,), (0,)), ((), ())), preferred_element_type=F32)
        even_t[:, pl.ds(pl.multiple_of(i * LANES, LANES), LANES)] = picked.astype(BF16)
        return 0

    lax.fori_loop(0, h, take_even, 0)

    @pl.when(is_top)
    def _():
        tiles[0] = jnp.zeros(tiles.shape[1:], BF16)

    @pl.when(is_bottom)
    def _():
        tiles[h + 1] = jnp.zeros(tiles.shape[1:], BF16)

    def make_spots(k, _):
        at = pl.ds(pl.multiple_of(k * LANES, LANES), LANES)
        for side, lane in ((0, half_cols - 1), (1, 0)):
            spots[side, :, at] = one_hot((LANES, LANES), lambda row, col: jnp.logical_and(row == k, col == lane))
        return 0

    lax.fori_loop(0, h + 2, make_spots, 0)

    def shifted_source(row, col):
        s, j = col // LANES, col % LANES
        return jnp.logical_and(row == j + 1 - s, j < half_cols)

    shift = one_hot((half_cols, 3 * LANES), shifted_source)

    for q, (lo, hi) in enumerate(spans):
        if q == 0:

            @pl.when(jnp.logical_not(is_top))
            def _():
                pltpu.make_async_copy(tiles.at[0], tiles.at[0], tile_recv.at[0]).wait()

        pltpu.make_async_copy(tiles.at[pl.ds(lo, hi - lo)], tiles.at[pl.ds(lo, hi - lo)], tile_recv.at[2 + q]).wait()
        if q == len(spans) - 1:

            @pl.when(jnp.logical_not(is_bottom))
            def _():
                pltpu.make_async_copy(tiles.at[h + 1], tiles.at[h + 1], tile_recv.at[1]).wait()

        block = tiles[pl.ds(q * group, group)].reshape(group * out_ch, half_cols)
        moved = jnp.dot(block, shift, preferred_element_type=F32).astype(BF16)
        for k in range(group):
            for s in range(3):
                taps[pl.ds(s * out_ch, out_ch), pl.ds((q * group + k) * LANES, LANES)] = moved[
                    k * out_ch:(k + 1) * out_ch, s * LANES:(s + 1) * LANES
                ]

    centre = taps[pl.ds(out_ch, out_ch), :]
    for side in range(2):
        edge_out[side] = lax.dot_general(
            centre, spots[side], (((1,), (1,)), ((), ())), preferred_element_type=F32
        ).astype(BF16)
    send(None, edge_out.at[0], edge_in.at[0], edge_send.at[0], edge_recv.at[0], {"lon": other("lon", 1)})
    send(None, edge_out.at[1], edge_in.at[1], edge_send.at[1], edge_recv.at[1], {"lon": other("lon", lon_n - 1)})

    def inject(s, came, spot):
        pltpu.make_async_copy(edge_in.at[came], edge_in.at[came], edge_recv.at[came]).wait()
        at = pl.ds(s * out_ch, out_ch)
        put = jnp.dot(edge_in[came], spots[spot], preferred_element_type=F32)
        taps[at, :] = (taps[at, :].astype(F32) + put).astype(BF16)

    counter = {"red": 0, "gat": 0, "land": 0}
    blocks = reduce_blocks(acc.shape[0], sizes)
    state = []

    def weight_terms(block):
        s = TAP_ORDER[block]
        for r in range(3):
            acc[pl.ds((3 * block + r) * in_ch, in_ch), :] = lax.dot_general(
                even_t[...], taps[pl.ds(s * out_ch, out_ch), pl.ds((2 - r) * LANES, h * LANES)],
                (((1,), (1,)), ((), ())), preferred_element_type=F32,
            )

    def owner_of(index, axis, owners):
        if owners == sizes[axis]:
            return None, index
        return index < owners, jnp.minimum(index, owners - 1)

    def scatter(block, stage):
        start, plan = blocks[block]
        axis, part, owners = plan[stage]
        base = start if stage == 0 else state[block]["base"]
        if stage == 0:
            state.append({"stack": []})
        land = landing[counter["land"]]
        counter["land"] += 1
        arrivals = []
        for d in range(1, sizes[axis]):
            p = other(axis, d)
            n = counter["red"]
            counter["red"] += 1
            toowner, target = owner_of(p, axis, owners)
            send(
                toowner, acc.at[pl.ds(pl.multiple_of(base + target * part, 8), part)], land.at[d - 1],
                red_send.at[n], red_recv.at[n], {axis: p},
            )
            arrivals.append(n)
        amowner, own = owner_of(me[axis], axis, owners)
        state[block]["base"] = base + own * part
        state[block]["stack"].append((axis, part, owners, base, amowner, own))
        state[block]["open"] = (land, arrivals, amowner, part)

    def add_up(block, final=False):
        land, arrivals, amowner, part = state[block]["open"]
        at = pl.ds(pl.multiple_of(state[block]["base"], 8), part)

        def absorb():
            for position, n in enumerate(arrivals):
                pltpu.make_async_copy(land.at[position], land.at[position], red_recv.at[n]).wait()
            total = acc[at, :]
            for position in range(len(arrivals)):
                total = total + land[position]
            if final:
                kg_out[at, :] = total * scale
            else:
                acc[at, :] = total

        if amowner is None:
            absorb()
        else:
            pl.when(amowner)(absorb)

    def gather(block, stage):
        axis, part, owners, base, amowner, own = state[block]["stack"][stage]
        at = pl.ds(pl.multiple_of(base + own * part, 8), part)
        waits = []
        for d in range(1, sizes[axis]):
            n = counter["gat"]
            counter["gat"] += 1
            send(amowner, kg_out.at[at], kg_out.at[at], gat_send.at[n], gat_recv.at[n], {axis: other(axis, d)})
            fromowner, source = owner_of(other(axis, sizes[axis] - d), axis, owners)
            there = kg_out.at[pl.ds(pl.multiple_of(base + source * part, 8), part)]
            waits.append((fromowner, pltpu.make_async_copy(there, there, gat_recv.at[n])))
        state[block]["waits"] = waits

    def gathered(block):
        for condition, copy in state[block]["waits"]:
            if condition is None:
                copy.wait()
            else:
                pl.when(condition)(lambda copy=copy: copy.wait())

    spread = one_hot((2 * half_cols, LANES), lambda row, col: row == 2 * col)

    def make_even_grad(i, _):
        total = jnp.zeros((in_ch, 2 * LANES), F32)
        for r in range(3):
            at = pl.ds(pl.multiple_of(i * 2 * LANES + (2 - r) * LANES, LANES), 2 * LANES)
            total = total + jnp.dot(kcat[r], taps[:, at], preferred_element_type=F32)
        total = total.astype(BF16)
        for k in range(2):
            row = lax.dot_general(
                spread, total[:, k * LANES:(k + 1) * LANES], (((1,), (1,)), ((), ())), preferred_element_type=F32
            )
            rows_buf[2 * i + k] = row.astype(BF16)
        return 0

    pairs = h // 2
    row_copies = []
    cuts = [pairs * k // 4 for k in range(5)]

    def even_grads(k):
        lax.fori_loop(cuts[k], cuts[k + 1], make_even_grad, 0)
        at = pl.ds(2 * cuts[k], 2 * (cuts[k + 1] - cuts[k]))
        copy = pltpu.make_async_copy(rows_buf.at[at], rows_out.at[at], row_sem.at[k])
        copy.start()
        row_copies.append(copy)

    weight_terms(0)
    scatter(0, 0)
    inject(0, 1, 0)
    add_up(0)
    scatter(0, 1)
    weight_terms(1)
    scatter(1, 0)
    inject(2, 0, 1)
    add_up(1)
    scatter(1, 1)
    add_up(0)
    scatter(0, 2)
    weight_terms(2)
    scatter(2, 0)
    for copy in local[1:]:
        copy.wait()
    add_up(2)
    scatter(2, 1)
    add_up(1)
    scatter(1, 2)
    even_grads(0)
    add_up(2)
    scatter(2, 2)
    for block in range(3):
        even_grads(block + 1)
        add_up(block, True)
        gather(block, 2)
    for stage in (1, 0):
        for block in range(3):
            gathered(block)
            gather(block, stage)
    for block in range(3):
        gathered(block)

    for copy in row_copies:
        copy.wait()
    for condition, copy in sends:
        if condition is None:
            copy.wait_send()
        else:
            pl.when(condition)(lambda copy=copy: copy.wait_send())


def group_size(slots):
    return max(size for size in range(1, 14) if slots % size == 0)


def reduce_blocks(rows, sizes):
    count = rows // 3
    return [(block * count, stage_plan(count, ("lat", "chan", "lon"), sizes)) for block in range(3)]


def finish_kernel(rows, kg_in, grad_out, kg_out, rows_buf, kg_buf, zeros, sems, kg_sems):
    zero_rows = zeros.shape[0]
    groups = rows.shape[0] // zero_rows
    kg_read = pltpu.make_async_copy(kg_in, kg_buf, sems.at[0])
    in_ch = kg_in.shape[0] // 9
    kg_writes = []
    for block in range(3):
        for r in range(3):
            kg_writes.append(
                pltpu.make_async_copy(
                    kg_buf.at[pl.ds((3 * block + r) * in_ch, in_ch)],
                    kg_out.at[pl.ds((3 * r + TAP_ORDER[block]) * in_ch, in_ch)],
                    kg_sems.at[3 * block + r],
                )
            )
    kg_read.start()
    reads, writes = [], list(kg_writes)
    for k in range(groups):
        at = pl.ds(k * zero_rows, zero_rows)
        reads.append(pltpu.make_async_copy(rows.at[at], rows_buf.at[at], sems.at[2 + 3 * k]))
        reads[k].start()
    zeros[...] = jnp.zeros(zeros.shape, BF16)
    for k in range(groups):
        at = pl.ds(k * zero_rows, zero_rows)
        writes.append(pltpu.make_async_copy(zeros, grad_out.at[at, 1], sems.at[3 + 3 * k]))
        writes[-1].start()
    kg_read.wait()
    for copy in kg_writes:
        copy.start()
    for k in range(groups):
        at = pl.ds(k * zero_rows, zero_rows)
        reads[k].wait()
        writes.append(pltpu.make_async_copy(rows_buf.at[at], grad_out.at[at, 0], sems.at[4 + 3 * k]))
        writes[-1].start()
    for copy in writes:
        copy.wait()


def on_device(sizes, fine_act, coarse_grad, kernel):
    fine_rows, fine_cols, in_ch = fine_act.shape
    out_ch = kernel.shape[3]
    h, w = fine_rows // 2, fine_cols // 2
    lon_n, lat_n, chan_n = (sizes[a] for a in AXES)
    scale = 1.0 / math.sqrt(h * lat_n * chan_n * w * lon_n)
    cg = jnp.transpose(coarse_grad, (0, 2, 1))
    fine = fine_act.reshape(h, 2, fine_cols, in_ch)
    blocks = reduce_blocks(9 * in_ch, sizes)
    landing, count = [], 0
    groups = (h + 2) // group_size(h + 2)
    for block, stage in ((0, 0), (0, 1), (1, 0), (1, 1), (0, 2), (2, 0), (2, 1), (1, 2), (2, 2)):
        axis, part, _ = blocks[block][1][stage]
        landing.append(pltpu.VMEM((sizes[axis] - 1, part, out_ch), F32))
        count += sizes[axis] - 1
    dma = pltpu.SemaphoreType.DMA
    vmem = pl.BlockSpec(memory_space=pltpu.VMEM)
    hbm = pl.BlockSpec(memory_space=pltpu.HBM)
    rows, kg = pl.pallas_call(
        functools.partial(grads_kernel, sizes, h, w, out_ch, scale),
        out_shape=(
            jax.ShapeDtypeStruct((h, fine_cols, in_ch), BF16),
            jax.ShapeDtypeStruct((9 * in_ch, out_ch), F32),
        ),
        in_specs=[hbm, hbm, hbm],
        out_specs=(hbm, vmem),
        scratch_shapes=[
            pltpu.VMEM((h, fine_cols, in_ch), BF16),
            pltpu.VMEM((3, in_ch, 3 * out_ch), BF16),
            pltpu.VMEM((h + 2, out_ch, w), BF16),
            pltpu.VMEM((3 * out_ch, (h + 2) * LANES), BF16),
            pltpu.VMEM((in_ch, h * LANES), BF16),
            pltpu.VMEM((2, out_ch, LANES), BF16),
            pltpu.VMEM((2, out_ch, LANES), BF16),
            pltpu.VMEM((2, LANES, (h + 2) * LANES), BF16),
            pltpu.VMEM((9 * in_ch, out_ch), F32),
            pltpu.VMEM((h, fine_cols, in_ch), BF16),
            dma((4,)),
            *landing,
            dma((10,)),
            dma((2 + groups,)),
            dma(((2 + groups) * (chan_n - 1) + 2,)),
            dma((2,)),
            dma((2,)),
            dma((count,)),
            dma((count,)),
            dma((count,)),
            dma((count,)),
        ],
        compiler_params=pltpu.CompilerParams(
            collective_id=0, has_side_effects=True, vmem_limit_bytes=60 * 1024 * 1024
        ),
        name="grads",
    )(fine, cg, kernel)
    zero_rows = math.gcd(h, 8)
    input_grad, kernel_grad = pl.pallas_call(
        finish_kernel,
        out_shape=(
            jax.ShapeDtypeStruct((h, 2, fine_cols, in_ch), BF16),
            jax.ShapeDtypeStruct(kg.shape, F32),
        ),
        in_specs=[hbm, hbm],
        out_specs=(hbm, hbm),
        scratch_shapes=[
            pltpu.VMEM((h, fine_cols, in_ch), BF16),
            pltpu.VMEM(kg.shape, F32),
            pltpu.VMEM((zero_rows, fine_cols, in_ch), BF16),
            dma((2 + 3 * (h // zero_rows),)),
            dma((9,)),
        ],
        compiler_params=pltpu.CompilerParams(vmem_limit_bytes=60 * 1024 * 1024),
        name="finish",
    )(rows, kg)
    return (input_grad.reshape(fine_act.shape), kernel_grad.reshape(3, 3, in_ch, out_ch))


def solution(mesh):
    placed = (P(("parts", "lat", "chan"), "lon", None), P(("parts", "lat"), "lon", "chan"), P())
    sizes = {axis: mesh.shape[axis] for axis in AXES}
    return jax.shard_map(
        functools.partial(on_device, sizes),
        mesh=mesh,
        in_specs=placed,
        out_specs=(P(("parts", "lat", "chan"), "lon", None), P("parts", None, None, None)),
        check_vma=False,
    )
```

profile of v0, /device:TPU:0, one launch (start us, length us, event | category | flops | bytes accessed | tf_op | source)
XLA Modules:
  0.0 54.1 jit_solution(9741358035615503043)
XLA Ops:
  0.6 48.8 %grads.1 = (bf16[24,224,256]{2,1,0:T(8,128)(2,1)}, f32[2304,128]{1,0:T(8,128)}) custom-call(bf16[24,2,224,256]{3,2,1,0:T(8,128)(2,1)} %bitcast.4, bf16[48,64,112]{2,1,0:T(8,128)(2,1)} %bitcast.5, bf16[3,3,256,128]{3,2,1,0:T(8,128)(2,1)} %kernel.1), custom_call_target="tpu_custom_call" | custom-call | tf_op jit(solution)/shard_map/grads/pallas_call | solution.py:428
  49.4 4.7 %finish.1 = (bf16[24,2,224,256]{3,2,1,0:T(8,128)(2,1)}, f32[2304,128]{1,0:T(8,128)}) custom-call(bf16[24,224,256]{2,1,0:T(8,128)(2,1)} %get-tuple-element.6.rows, f32[2304,128]{1,0:T(8,128)} %get-tuple-element.7.kg_in), custom_call_target="tpu_custom_call" | custom-call | tf_op jit(solution)/shard_map/finish/pallas_call | solution.py:465
where the time goes:
time: 54.2 us; the launch traced here: 54.1 us
  Pallas kernels  53.5 us (99%)
  between operations  0.64 us (1%)
    pallas_call x1, Pallas kernels, on_device(): pl.pallas_call(functools.partial(grads_kernel, sizes, h, w, out_ch, scale...  48.8 us
    pallas_call x1, Pallas kernels, on_device(): pl.pallas_call(finish_kernel, out_shape=(jax.ShapeDtypeStruct((h, 2, fine...  4.68 us

commit v1 on v0

--- a/solution.py
+++ b/solution.py
@@ -44,7 +44,7 @@
 def grads_kernel(
     sizes, half_rows, half_cols, out_ch, scale,
     fine, cg, kernel, rows_out, kg_out,
-    fbuf, kcat, tiles, taps, even_t, edge_out, edge_in, spots, acc, rows_buf, row_sem, *rest,
+    fbuf, kcat, tiles, taps, even_t, edge_out, edge_in, spots, acc, row_sem, *rest,
 ):
     landing, (local_sem, tile_recv, tile_send, edge_send, edge_recv, red_send, red_recv, gat_send, gat_recv) = rest[:-9], rest[-9:]
     lon_n, lat_n, chan_n = (sizes[a] for a in AXES)
@@ -303,7 +303,7 @@
             row = lax.dot_general(
                 spread, total[:, k * LANES:(k + 1) * LANES], (((1,), (1,)), ((), ())), preferred_element_type=F32
             )
-            rows_buf[2 * i + k] = row.astype(BF16)
+            rows_out[2 * i + k] = row.astype(BF16)
         return 0
 
     pairs = h // 2
@@ -312,10 +312,6 @@
 
     def even_grads(k):
         lax.fori_loop(cuts[k], cuts[k + 1], make_even_grad, 0)
-        at = pl.ds(2 * cuts[k], 2 * (cuts[k + 1] - cuts[k]))
-        copy = pltpu.make_async_copy(rows_buf.at[at], rows_out.at[at], row_sem.at[k])
-        copy.start()
-        row_copies.append(copy)
 
     weight_terms(0)
     scatter(0, 0)
@@ -369,39 +365,29 @@
     return [(block * count, stage_plan(count, ("lat", "chan", "lon"), sizes)) for block in range(3)]
 
 
-def finish_kernel(rows, kg_in, grad_out, kg_out, rows_buf, kg_buf, zeros, sems, kg_sems):
+def finish_kernel(rows, kg_in, grad_out, kg_out, zeros, sems, kg_sems):
     zero_rows = zeros.shape[0]
     groups = rows.shape[0] // zero_rows
-    kg_read = pltpu.make_async_copy(kg_in, kg_buf, sems.at[0])
     in_ch = kg_in.shape[0] // 9
-    kg_writes = []
+    writes = []
+    for k in range(groups):
+        at = pl.ds(k * zero_rows, zero_rows)
+        writes.append(pltpu.make_async_copy(rows.at[at], grad_out.at[at, 0], sems.at[4 + 3 * k]))
     for block in range(3):
         for r in range(3):
-            kg_writes.append(
+            writes.append(
                 pltpu.make_async_copy(
-                    kg_buf.at[pl.ds((3 * block + r) * in_ch, in_ch)],
+                    kg_in.at[pl.ds((3 * block + r) * in_ch, in_ch)],
                     kg_out.at[pl.ds((3 * r + TAP_ORDER[block]) * in_ch, in_ch)],
                     kg_sems.at[3 * block + r],
                 )
             )
-    kg_read.start()
-    reads, writes = [], list(kg_writes)
-    for k in range(groups):
-        at = pl.ds(k * zero_rows, zero_rows)
-        reads.append(pltpu.make_async_copy(rows.at[at], rows_buf.at[at], sems.at[2 + 3 * k]))
-        reads[k].start()
+    for c in writes:
+        c.start()
     zeros[...] = jnp.zeros(zeros.shape, BF16)
     for k in range(groups):
         at = pl.ds(k * zero_rows, zero_rows)
         writes.append(pltpu.make_async_copy(zeros, grad_out.at[at, 1], sems.at[3 + 3 * k]))
-        writes[-1].start()
-    kg_read.wait()
-    for copy in kg_writes:
-        copy.start()
-    for k in range(groups):
-        at = pl.ds(k * zero_rows, zero_rows)
-        reads[k].wait()
-        writes.append(pltpu.make_async_copy(rows_buf.at[at], grad_out.at[at, 0], sems.at[4 + 3 * k]))
         writes[-1].start()
     for copy in writes:
         copy.wait()
@@ -428,11 +414,11 @@
     rows, kg = pl.pallas_call(
         functools.partial(grads_kernel, sizes, h, w, out_ch, scale),
         out_shape=(
-            jax.ShapeDtypeStruct((h, fine_cols, in_ch), BF16),
-            jax.ShapeDtypeStruct((9 * in_ch, out_ch), F32),
+            pltpu.VMEM((h, fine_cols, in_ch), BF16),
+            pltpu.VMEM((9 * in_ch, out_ch), F32),
         ),
         in_specs=[hbm, hbm, hbm],
-        out_specs=(hbm, vmem),
+        out_specs=(vmem, vmem),
         scratch_shapes=[
             pltpu.VMEM((h, fine_cols, in_ch), BF16),
             pltpu.VMEM((3, in_ch, 3 * out_ch), BF16),
@@ -443,7 +429,6 @@
             pltpu.VMEM((2, out_ch, LANES), BF16),
             pltpu.VMEM((2, LANES, (h + 2) * LANES), BF16),
             pltpu.VMEM((9 * in_ch, out_ch), F32),
-            pltpu.VMEM((h, fine_cols, in_ch), BF16),
             dma((4,)),
             *landing,
             dma((10,)),
@@ -468,16 +453,14 @@
             jax.ShapeDtypeStruct((h, 2, fine_cols, in_ch), BF16),
             jax.ShapeDtypeStruct(kg.shape, F32),
         ),
-        in_specs=[hbm, hbm],
+        in_specs=[vmem, vmem],
         out_specs=(hbm, hbm),
         scratch_shapes=[
-            pltpu.VMEM((h, fine_cols, in_ch), BF16),
-            pltpu.VMEM(kg.shape, F32),
             pltpu.VMEM((zero_rows, fine_cols, in_ch), BF16),
             dma((2 + 3 * (h // zero_rows),)),
             dma((9,)),
         ],
-        compiler_params=pltpu.CompilerParams(vmem_limit_bytes=60 * 1024 * 1024),
+        compiler_params=pltpu.CompilerParams(vmem_limit_bytes=40 * 1024 * 1024),
         name="finish",
     )(rows, kg)
     return (input_grad.reshape(fine_act.shape), kernel_grad.reshape(3, 3, in_ch, out_ch))

time: 54.2 us -> 51.5 us (0.950)
  Pallas kernels: 53.5 us -> 50.7 us
    pallas_call x1, Pallas kernels: 4.68 us -> 2.97 us  [on_device(): pl.pallas_call(finish_kernel, out_shape=(jax.ShapeDtypeStruct((h, 2, fine...]
    pallas_call x1, Pallas kernels: 48.8 us -> 47.8 us  [on_device(): pl.pallas_call(functools.partial(grads_kernel, sizes, h, w, out_ch, scale...]
where the time goes in v1:
time: 51.5 us; the launch traced here: 51.4 us
  Pallas kernels  50.7 us (98%)
  between operations  0.64 us (1%)
    pallas_call x1, Pallas kernels, on_device(): pl.pallas_call(functools.partial(grads_kernel, sizes, h, w, out_ch, scale...  47.8 us
    pallas_call x1, Pallas kernels, on_device(): pl.pallas_call(finish_kernel, out_shape=(jax.ShapeDtypeStruct((h, 2, fine...  2.97 us

profile of v1, /device:TPU:0, one launch (start us, length us, event | category | flops | bytes accessed | tf_op | source)
XLA Modules:
  0.0 51.4 jit_solution(17386684693426997774)
XLA Ops:
  0.6 47.8 %grads.1 = (bf16[24,224,256]{2,1,0:T(8,128)(2,1)S(1)}, f32[2304,128]{1,0:T(8,128)S(1)}) custom-call(bf16[24,2,224,256]{3,2,1,0:T(8,128)(2,1)} %bitcast.4, bf16[48,64,112]{2,1,0:T(8,128)(2,1)} %bitcast.5, bf16[3,3,256,128]{3,2,1,0:T(8,128)(2,1)} %kernel.1), custom_call_target="tpu_custom_call" | custom-call | tf_op jit(solution)/shard_map/grads/pallas_call | solution.py:414
  48.4 3.0 %finish.1 = (bf16[24,2,224,256]{3,2,1,0:T(8,128)(2,1)}, f32[2304,128]{1,0:T(8,128)}) custom-call(bf16[24,224,256]{2,1,0:T(8,128)(2,1)S(1)} %get-tuple-element.6.rows, f32[2304,128]{1,0:T(8,128)S(1)} %get-tuple-element.7.kg_in), custom_call_target="tpu_custom_call" | custom-call | tf_op jit(solution)/shard_map/finish/pallas_call | solution.py:450

commit v2 on v1

v2 whole, which is shorter than its diff:
```python
import functools
import math

import jax
import jax.numpy as jnp
from jax import lax
from jax.experimental import pallas as pl
from jax.experimental.pallas import tpu as pltpu
from jax.sharding import PartitionSpec as P

MESH = pl.DeviceIdType.MESH
LANES = 128
PACK = 16
F32 = jnp.float32
BF16 = jnp.bfloat16
AXES = ("lon", "lat", "chan")
VMEM_BYTES = 67043328


def one_hot(shape, test):
    rows = lax.broadcasted_iota(jnp.int32, shape, 0)
    cols = lax.broadcasted_iota(jnp.int32, shape, 1)
    return jnp.where(test(rows, cols), 1.0, 0.0).astype(BF16)


def share(rows, peers, unit):
    for size in range(unit, rows + 1, unit):
        if rows % size == 0 and rows // size <= peers:
            return size
    raise ValueError("no share")


class Plan:
    def __init__(self, sizes, fine_shape, cg_shape, kernel_shape):
        self.lon_n, self.lat_n, self.chan_n = (sizes[a] for a in AXES)
        self.h, self.w = fine_shape[0] // 2, fine_shape[1] // 2
        self.in_ch, self.out_ch = kernel_shape[2], kernel_shape[3]
        self.width = cg_shape[2]
        self.group = min(self.width, 32)
        self.units = self.width // self.group
        self.part = share(3 * self.group, self.lon_n, 8)
        self.owners = 3 * self.group // self.part
        self.cut = self.in_ch // self.lat_n
        self.fine_cuts = 4 if self.h % 4 == 0 else 1
        parcels = 3 + (self.chan_n - 1) * self.units
        self.remote = (
            2 + 2 + 2
            + (self.chan_n - 1) * (self.units + 1)
            + parcels * (self.lat_n + self.lon_n + 1)
            + self.units * (self.lon_n - 1)
            + self.units * self.lon_n * (self.chan_n - 1)
            + self.chan_n * self.units * (self.lat_n - 1)
        )


def grads_kernel(
    plan, scale,
    fine, cg, kernel, rows_out, kg_out,
    fbuf, kcat, tiles, xs, ev, tt, edge_out, edge_in, tedge_out, tedge_in,
    acc, land_lat, land_lon, land_x,
    fine_sem, kernel_sem, own_sem, halo_recv, send_sem, recv_sem,
):
    lon_n, lat_n, chan_n = plan.lon_n, plan.lat_n, plan.chan_n
    h, w, width, group, units = plan.h, plan.w, plan.width, plan.group, plan.units
    part, owners, out_ch, cut = plan.part, plan.owners, plan.out_ch, plan.cut
    sizes = {"lon": lon_n, "lat": lat_n, "chan": chan_n}
    me = {a: lax.axis_index(a) for a in AXES}
    lon, lat, chan = me["lon"], me["lat"], me["chan"]
    my_chunk = jnp.minimum(lon, owners - 1)
    is_owner = None if owners == lon_n else lon < owners

    def other(axis, step):
        return lax.rem(me[axis] + step + sizes[axis], sizes[axis])

    def channels(block, unit=0, size=None):
        start = pl.multiple_of(block * width + unit * group, PACK)
        return pl.ds(start, width if size is None else size)

    def guarded(condition, action):
        if condition is None:
            action()
        else:
            pl.when(condition)(action)

    step = h // plan.fine_cuts
    fine_in = []
    for k in range(plan.fine_cuts):
        at = pl.ds(k * step, step)
        fine_in.append(pltpu.make_async_copy(fine.at[at, 0], fbuf.at[at], fine_sem.at[k]))

    def first_row(p):
        return jnp.maximum(p * h - 1, 0), jnp.where(p > 0, 0, 1)

    own_from, own_to = first_row(chan)
    own_in = pltpu.make_async_copy(
        cg.at[pl.ds(own_from, h + 1)], tiles.at[pl.ds(own_to, h + 1), channels(chan)], own_sem.at[0]
    )
    inner = jnp.logical_and(chan > 0, chan < chan_n - 1)
    own_extra = pltpu.make_async_copy(
        cg.at[jnp.minimum((chan + 1) * h, chan_n * h - 1)], tiles.at[h + 1, channels(chan)], own_sem.at[1]
    )
    kernel_in = []
    for r in range(3):
        for s in range(3):
            n = 3 * r + s
            kernel_in.append(
                pltpu.make_async_copy(kernel.at[r, s], kcat.at[:, pl.ds(n * out_ch, out_ch)], kernel_sem.at[n])
            )
    barrier = pltpu.get_barrier_semaphore()
    greeted = 0
    for dl in range(lat_n):
        for dc in range(chan_n):
            if dl or dc:
                pl.semaphore_signal(
                    barrier, inc=1, device_id={"lat": other("lat", dl), "chan": other("chan", dc)}, device_id_type=MESH
                )
                greeted += 1
    for d in range(1, lon_n):
        pl.semaphore_signal(barrier, inc=1, device_id={"lon": other("lon", d)}, device_id_type=MESH)
        greeted += 1

    for copy in fine_in:
        copy.start()
    own_in.start()
    if chan_n > 2:
        pl.when(inner)(lambda: own_extra.start())
    for copy in kernel_in:
        copy.start()

    is_top = jnp.logical_and(lat == 0, chan == 0)
    is_bottom = jnp.logical_and(lat == lat_n - 1, chan == chan_n - 1)

    @pl.when(is_top)
    def _():
        tiles[0] = jnp.zeros(tiles.shape[1:], BF16)

    @pl.when(is_bottom)
    def _():
        tiles[h + 1] = jnp.zeros(tiles.shape[1:], BF16)

    def picked_column(row, col):
        s, j = row // LANES, row % LANES
        return jnp.logical_and(jnp.logical_and(col == 2 * (j + s - 1), j < w), col >= 0)

    pick = one_hot((3 * LANES, 2 * w), picked_column)

    def take_even(i, _):
        picked = jnp.dot(pick, fbuf[i], preferred_element_type=F32)
        at = pl.ds(pl.multiple_of(i * LANES, LANES), LANES)
        for s in range(3):
            ev[s, at, :] = picked[s * LANES:(s + 1) * LANES].astype(BF16)
        edge_out[0, pl.ds(i, 1), :] = picked[LANES + w - 1:LANES + w]
        edge_out[1, pl.ds(i, 1), :] = picked[LANES:LANES + 1]
        return 0

    for k in range(plan.fine_cuts):
        fine_in[k].wait()
        lax.fori_loop(k * step, (k + 1) * step, take_even, 0)

    pad = jnp.zeros((width, LANES - w), BF16) if w < LANES else None

    def fill(d, unit, size, which):
        at = pl.ds(d * width + unit * group, size)
        source = channels(other("chan", d), unit, size)
        for i in which:
            block = tiles[i, source, :]
            if pad is not None:
                block = jnp.concatenate([block, pad[:size]], axis=1)
            xs[at, pl.ds(i * LANES, LANES)] = block

    own_in.wait()
    if chan_n > 2:
        pl.when(inner)(lambda: own_extra.wait())
    fill(0, 0, width, range(1, h + 1))

    pl.semaphore_wait(barrier, greeted)

    sends = []

    def send(condition, src, dst, where, recv=None):
        n = len(sends)
        copy = pltpu.make_async_remote_copy(
            src_ref=src, dst_ref=dst, send_sem=send_sem.at[n], recv_sem=recv_sem.at[n] if recv is None else recv,
            device_id=where, device_id_type=MESH,
        )
        guarded(condition, lambda: copy.start())
        sends.append((condition, copy))
        return n

    def arrive(ref, n, condition=None):
        guarded(condition, lambda: pltpu.make_async_copy(ref, ref, recv_sem.at[n]).wait())

    def both(a, b):
        return b if a is None else a if b is None else jnp.logical_and(a, b)

    send(
        lat < lat_n - 1, cg.at[chan_n * h - 1], tiles.at[0, channels(chan)],
        {"lat": jnp.minimum(lat + 1, lat_n - 1), "chan": 0}, halo_recv.at[chan],
    )
    send(
        lat > 0, cg.at[0], tiles.at[h + 1, channels(chan)],
        {"lat": jnp.maximum(lat - 1, 0), "chan": chan_n - 1}, halo_recv.at[chan_n + chan],
    )
    edge_n = [
        send(None, edge_out.at[0], edge_in.at[0], {"lon": other("lon", 1)}),
        send(None, edge_out.at[1], edge_in.at[1], {"lon": other("lon", -1)}),
    ]
    tile_n = {}
    for d in range(1, chan_n):
        p = other("chan", -d)
        source, target = first_row(p)
        for u in range(units):
            tile_n[d, u] = send(
                None, cg.at[pl.ds(source, h + 1), pl.ds(u * group, group)],
                tiles.at[pl.ds(target, h + 1), channels(chan, u, group)], {"chan": p},
            )
        if chan_n > 2:
            tile_n[d] = send(
                jnp.logical_and(p > 0, p < chan_n - 1), cg.at[jnp.minimum((p + 1) * h, chan_n * h - 1)],
                tiles.at[h + 1, channels(chan)], {"chan": p},
            )

    def halo_arrive(d):
        block = other("chan", d)
        for row, n, condition in (
            (0, block, jnp.logical_and(chan == 0, lat > 0)),
            (h + 1, chan_n + block, jnp.logical_and(chan == chan_n - 1, lat < lat_n - 1)),
        ):
            ref = tiles.at[row, channels(block)]
            guarded(condition, lambda: pltpu.make_async_copy(ref, ref, halo_recv.at[n]).wait())

    def tiles_arrive(d, u):
        block = other("chan", d)
        _, target = first_row(chan)
        arrive(tiles.at[pl.ds(target, h + 1), channels(block, u, group)], tile_n[d, u])
        if u == 0:
            if chan_n > 2:
                arrive(tiles.at[h + 1, channels(block)], tile_n[d], inner)
            halo_arrive(d)

    def terms(d, first, count, s):
        pieces = []
        for u in range(first, first + count):
            for r in range(3):
                pieces.append(xs[pl.ds(d * width + u * group, group), pl.ds((2 - r) * LANES, h * LANES)])
        total = jnp.dot(jnp.concatenate(pieces, axis=0), ev[s], preferred_element_type=F32)
        for u in range(count):
            for k in range(owners):
                at = (u * owners + k) * part
                for half in range(lat_n):
                    acc[half, d * units + first + u, k, s] = total[at:at + part, half * cut:(half + 1) * cut]

    def lat_send(d, first, count, s0, s_n):
        g, s = pl.ds(d * units + first, count), pl.ds(s0, s_n)
        numbers = []
        for dl in range(1, lat_n):
            l = other("lat", dl)
            numbers.append(
                send(None, acc.at[l, g, :, s], land_lat.at[dl - 1, g, :, s], {"lat": l})
            )
        return numbers

    def lat_add(parcel, numbers):
        d, first, count, s0, s_n = parcel
        g, s = pl.ds(d * units + first, count), pl.ds(s0, s_n)
        for dl in range(1, lat_n):
            arrive(land_lat.at[dl - 1, g, :, s], numbers[dl - 1])
        total = acc[lat, g, :, s]
        for dl in range(1, lat_n):
            total = total + land_lat[dl - 1, g, :, s]
        acc[lat, g, :, s] = total
        result = []
        for dz in range(1, lon_n):
            k = other("lon", dz)
            result.append(
                send(
                    None if owners == lon_n else k < owners, acc.at[lat, g, jnp.minimum(k, owners - 1), s],
                    land_lon.at[dz - 1, g, s], {"lon": k},
                )
            )
        return result

    x_n = {}

    def lon_sum(parcel, numbers):
        d, first, count, s0, s_n = parcel
        g, s = pl.ds(d * units + first, count), pl.ds(s0, s_n)
        for dz in range(1, lon_n):
            arrive(land_lon.at[dz - 1, g, s], numbers[dz - 1], is_owner)
        total = acc[lat, g, my_chunk, s]
        for dz in range(1, lon_n):
            total = total + land_lon[dz - 1, g, s]
        return total

    def lon_add(parcel, numbers):
        d, first, count, s0, s_n = parcel
        g, s = pl.ds(d * units + first, count), pl.ds(s0, s_n)

        def add():
            acc[lat, g, my_chunk, s] = lon_sum(parcel, numbers)

        guarded(is_owner, add)
        x_n[parcel] = send(
            is_owner, acc.at[lat, g, my_chunk, s], land_x.at[d, pl.ds(first, count), s], {"chan": other("chan", d + 1)}
        )

    last = chan_n - 1
    mine = other("chan", last)
    z_n, fx_n, lat_n_of = {}, {}, {}

    def owner_of(dz):
        k = other("lon", -dz)
        return jnp.minimum(k, owners - 1), (None if owners == lon_n else k < owners)

    def forward(u, dz):
        k, there = owner_of(dz)
        at = kg_out.at[lat, mine, u, k]
        for e in range(1, chan_n):
            fx_n[u, dz, e] = send(there, at, at, {"chan": other("chan", e)})

    def finish(parcel, numbers):
        u = parcel[1]

        def add():
            total = lon_sum(parcel, numbers)
            for other_parcel, n in x_n.items():
                d, first, count, s0, s_n = other_parcel
                if first <= u < first + count and n not in done:
                    ref = land_x.at[d, pl.ds(first, count), pl.ds(s0, s_n)]
                    pltpu.make_async_copy(ref, ref, recv_sem.at[n]).wait()
                    done.append(n)
            total = total[0]
            for d in range(last):
                total = total + land_x[d, u]
            kg_out[lat, mine, u, my_chunk] = total * scale

        guarded(is_owner, add)
        at = kg_out.at[lat, mine, u, my_chunk]
        for dz in range(1, lon_n):
            z_n[u, dz] = send(is_owner, at, at, {"lon": other("lon", dz)})
        forward(u, 0)

    done = []

    def relay(u):
        for dz in range(1, lon_n):
            k, there = owner_of(dz)
            arrive(kg_out.at[lat, mine, u, k], z_n[u, dz], there)
            forward(u, dz)
        lat_forward(mine, u)

    def lat_forward(block, u):
        at = kg_out.at[lat, block, u]
        for dl in range(1, lat_n):
            n = send(None, at, at, {"lat": other("lat", dl)})
            lat_n_of[len(lat_n_of)] = (n, dl, block, u)

    def collect(u):
        for e in range(1, chan_n):
            block = other("chan", -e - 1)
            for dz in range(lon_n):
                k, there = owner_of(dz)
                arrive(kg_out.at[lat, block, u, k], fx_n[u, dz, e], there)
            lat_forward(block, u)

    def turned(row, col):
        s, j = row // w, row % w
        return col == j + 1 - s

    def make_taps():
        turn = one_hot((3 * w, w), turned)
        for i in range(0, h + 2, 2):
            pair = tiles[pl.ds(i, 2)].reshape(2 * out_ch, w)
            moved = lax.dot_general(turn, pair, (((1,), (1,)), ((), ())), preferred_element_type=F32)
            for k in range(2):
                lanes = slice(k * out_ch, (k + 1) * out_ch)
                for s in range(3):
                    tt[s, pl.ds((i + k) * w, w), :] = moved[s * w:(s + 1) * w, lanes].astype(BF16)
                tedge_out[0, pl.ds(i + k, 1), :] = moved[2 * w - 1:2 * w, lanes]
                tedge_out[1, pl.ds(i + k, 1), :] = moved[w:w + 1, lanes]

    def patch(buffer, base, row, value):
        start = base + row // PACK * PACK
        at = pl.ds(pl.multiple_of(start, PACK), PACK)
        old = buffer[at, :].astype(F32)
        rows = lax.broadcasted_iota(jnp.int32, old.shape, 0)
        buffer[at, :] = jnp.where(rows == row % PACK, value, old).astype(BF16)

    def patch_even(i, _):
        base = i * LANES
        patch(ev.at[0], base, 0, edge_in[0, pl.ds(i, 1), :])
        patch(ev.at[2], base, w - 1, edge_in[1, pl.ds(i, 1), :])
        return 0

    def patch_taps(i, _):
        base = i * w
        patch(tt.at[2], base, 0, tedge_in[0, pl.ds(i, 1), :])
        patch(tt.at[0], base, w - 1, tedge_in[1, pl.ds(i, 1), :])
        return 0

    ig_rows = math.gcd(h, 4)
    spread = one_hot((2 * w, w), lambda row, col: row == 2 * col)

    def even_grads(b, _):
        pieces = []
        for r in range(3):
            at = pl.ds(pl.multiple_of((b * ig_rows + 2 - r) * w, PACK), ig_rows * w)
            for s in range(3):
                pieces.append(tt[s, at, :])
        total = lax.dot_general(
            jnp.concatenate(pieces, axis=1), kcat[...], (((1,), (1,)), ((), ())), preferred_element_type=F32
        ).astype(BF16)
        for k in range(ig_rows):
            row = jnp.dot(spread, total[k * w:(k + 1) * w], preferred_element_type=F32)
            rows_out[b * ig_rows + k] = row.astype(BF16)
        return 0

    blocks = h // ig_rows
    state = {"ig": 0}

    def some_even_grads(count):
        end = min(blocks, state["ig"] + count)
        if end > state["ig"]:
            lax.fori_loop(state["ig"], end, even_grads, 0)
        state["ig"] = end

    halo_arrive(0)
    fill(0, 0, width, (0, h + 1))
    parcels = {}

    def begin(d, first, count, s0, s_n):
        parcel = (d, first, count, s0, s_n)
        for s in range(s0, s0 + s_n):
            terms(d, first, count, s)
        parcels[parcel] = lat_send(*parcel)
        return parcel

    a1 = begin(0, 0, units, 1, 1)
    for n, ref in zip(edge_n, (edge_in.at[0], edge_in.at[1])):
        arrive(ref, n)
    lax.fori_loop(0, h, patch_even, 0)
    parcels[a1] = lat_add(a1, parcels[a1])
    a0 = begin(0, 0, units, 0, 1)
    a2 = begin(0, 0, units, 2, 1)
    parcels[a0] = lat_add(a0, parcels[a0])
    parcels[a2] = lat_add(a2, parcels[a2])
    own = [a1, a0, a2]
    early = []
    for d in range(1, chan_n):
        for u in range(units):
            tiles_arrive(d, u)
            fill(d, u, group, range(h + 2))
            parcel = begin(d, u, 1, 0, 3)
            early.append(parcel)
            parcels[parcel] = lat_add(parcel, parcels[parcel])
    for parcel in own + [q for q in early if q[0] < last]:
        lon_add(parcel, parcels[parcel])
    make_taps()
    tedge_n = [
        send(None, tedge_out.at[0], tedge_in.at[0], {"lon": other("lon", 1)}),
        send(None, tedge_out.at[1], tedge_in.at[1], {"lon": other("lon", -1)}),
    ]
    finals = [q for q in early if q[0] == last]
    for copy in kernel_in:
        copy.wait()
    for n, ref in zip(tedge_n, (tedge_in.at[0], tedge_in.at[1])):
        arrive(ref, n)
    lax.fori_loop(0, h + 2, patch_taps, 0)
    for k, parcel in enumerate(finals):
        finish(parcel, parcels[parcel])
        some_even_grads(blocks // (2 * len(finals)))
    for k, parcel in enumerate(finals):
        relay(parcel[1])
        some_even_grads(-(-blocks // (2 * len(finals))))
    some_even_grads(blocks)
    for parcel in finals:
        collect(parcel[1])
    for n, dl, block, u in lat_n_of.values():
        there = other("lat", -dl)
        arrive(kg_out.at[there, block, u], n)
    for condition, copy in sends:
        guarded(condition, lambda: copy.wait_send())


def finish_kernel(plan, rows, kg_in, grad_out, kg_out, zeros, turned, sems, kg_sems):
    zero_rows = zeros.shape[0]
    groups = rows.shape[0] // zero_rows
    in_ch, part, group, cut = plan.in_ch, plan.part, plan.group, plan.cut
    writes = []
    for k in range(groups):
        at = pl.ds(k * zero_rows, zero_rows)
        writes.append(pltpu.make_async_copy(rows.at[at], grad_out.at[at, 0], sems.at[2 * k]))
        writes[-1].start()
    zeros[...] = jnp.zeros(zeros.shape, BF16)
    for k in range(groups):
        at = pl.ds(k * zero_rows, zero_rows)
        writes.append(pltpu.make_async_copy(zeros, grad_out.at[at, 1], sems.at[2 * k + 1]))
        writes[-1].start()
    for s in range(3):
        for half in range(plan.lat_n):
            pieces = [[], [], []]
            for p in range(plan.chan_n):
                for u in range(plan.units):
                    stack = jnp.concatenate([kg_in[half, p, u, k, s] for k in range(plan.owners)], axis=0)
                    for r in range(3):
                        pieces[r].append(stack[r * group:(r + 1) * group])
            for r in range(3):
                turned[3 * r + s, pl.ds(half * cut, cut), :] = jnp.concatenate(pieces[r], axis=0).T
        for r in range(3):
            n = 3 * r + s
            writes.append(
                pltpu.make_async_copy(turned.at[n], kg_out.at[pl.ds(n * in_ch, in_ch)], kg_sems.at[n])
            )
            writes[-1].start()
    for copy in writes:
        copy.wait()


def on_device(sizes, fine_act, coarse_grad, kernel):
    plan = Plan(sizes, fine_act.shape, coarse_grad.shape, kernel.shape)
    fine_rows, fine_cols, in_ch = fine_act.shape
    h, w, out_ch = plan.h, plan.w, plan.out_ch
    scale = 1.0 / math.sqrt(h * plan.lat_n * plan.chan_n * w * plan.lon_n)
    cg = jnp.transpose(coarse_grad, (0, 2, 1))
    fine = fine_act.reshape(h, 2, fine_cols, in_ch)
    dma = pltpu.SemaphoreType.DMA
    vmem = pl.BlockSpec(memory_space=pltpu.VMEM)
    hbm = pl.BlockSpec(memory_space=pltpu.HBM)
    sums = plan.chan_n * plan.units
    chunk = (3, plan.part, plan.cut)
    rows_shape = (h, fine_cols, in_ch)
    kg_shape = (plan.lat_n, plan.chan_n, plan.units, plan.owners) + chunk
    edge_rows = -(-(h + 2) // 8) * 8
    held = 2 * math.prod(rows_shape) + 4 * math.prod(kg_shape)
    rows, kg = pl.pallas_call(
        functools.partial(grads_kernel, plan, scale),
        out_shape=(pltpu.VMEM(rows_shape, BF16), pltpu.VMEM(kg_shape, F32)),
        in_specs=[hbm, hbm, hbm],
        out_specs=(vmem, vmem),
        scratch_shapes=[
            pltpu.VMEM((h, fine_cols, in_ch), BF16),
            pltpu.VMEM((in_ch, 9 * out_ch), BF16),
            pltpu.VMEM((h + 2, out_ch, w), BF16),
            pltpu.VMEM((out_ch, (h + 2) * LANES), BF16),
            pltpu.VMEM((3, h * LANES, in_ch), BF16),
            pltpu.VMEM((3, (h + 2) * w, out_ch), BF16),
            pltpu.VMEM((2, edge_rows, in_ch), F32),
            pltpu.VMEM((2, edge_rows, in_ch), F32),
            pltpu.VMEM((2, edge_rows, out_ch), F32),
            pltpu.VMEM((2, edge_rows, out_ch), F32),
            pltpu.VMEM((plan.lat_n, sums, plan.owners) + chunk, F32),
            pltpu.VMEM((plan.lat_n - 1, sums, plan.owners) + chunk, F32),
            pltpu.VMEM((plan.lon_n - 1, sums) + chunk, F32),
            pltpu.VMEM((plan.chan_n - 1, plan.units) + chunk, F32),
            dma((plan.fine_cuts,)),
            dma((9,)),
            dma((2,)),
            dma((2 * plan.chan_n,)),
            dma((plan.remote,)),
            dma((plan.remote,)),
        ],
        compiler_params=pltpu.CompilerParams(
            collective_id=0, has_side_effects=True, vmem_limit_bytes=(VMEM_BYTES - held) // 65536 * 65536
        ),
        name="grads",
    )(fine, cg, kernel)
    zero_rows = math.gcd(h, 8)
    input_grad, kernel_grad = pl.pallas_call(
        functools.partial(finish_kernel, plan),
        out_shape=(
            jax.ShapeDtypeStruct((h, 2, fine_cols, in_ch), BF16),
            jax.ShapeDtypeStruct((9 * in_ch, out_ch), F32),
        ),
        in_specs=[vmem, vmem],
        out_specs=(hbm, hbm),
        scratch_shapes=[
            pltpu.VMEM((zero_rows, fine_cols, in_ch), BF16),
            pltpu.VMEM((9, in_ch, out_ch), F32),
            dma((2 * (h // zero_rows),)),
            dma((9,)),
        ],
        compiler_params=pltpu.CompilerParams(vmem_limit_bytes=VMEM_BYTES // 4),
        name="finish",
    )(rows, kg)
    return (input_grad.reshape(fine_act.shape), kernel_grad.reshape(3, 3, in_ch, out_ch))


def solution(mesh):
    placed = (P(("parts", "lat", "chan"), "lon", None), P(("parts", "lat"), "lon", "chan"), P())
    sizes = {axis: mesh.shape[axis] for axis in AXES}
    return jax.shard_map(
        functools.partial(on_device, sizes),
        mesh=mesh,
        in_specs=placed,
        out_specs=(P(("parts", "lat", "chan"), "lon", None), P("parts", None, None, None)),
        check_vma=False,
    )
```

time: 51.5 us -> 45.9 us (0.89)
  Pallas kernels: 50.7 us -> 45.1 us
    pallas_call x2, Pallas kernels: 50.7 us -> 45.1 us  [the longest x1 42 us: on_device(): pl.pallas_call(functools.partial(grads_kernel, plan, scale), out_shape=(p...]
where the time goes in v2:
time: 45.9 us; the launch traced here: 45.7 us
  Pallas kernels  45.1 us (98%)
  between operations  0.64 us (1%)
    pallas_call x1, Pallas kernels, on_device(): pl.pallas_call(functools.partial(grads_kernel, plan, scale), out_shape=(p...  42 us
    pallas_call x1, Pallas kernels, on_device(): pl.pallas_call(functools.partial(finish_kernel, plan), out_shape=(jax.Sha...  3.05 us

profile of v2, /device:TPU:0, one launch (start us, length us, event | category | flops | bytes accessed | tf_op | source)
XLA Modules:
  0.0 45.7 jit_solution(10014292721698143126)
XLA Ops:
  0.6 42.0 %grads.1 = (bf16[24,224,256]{2,1,0:T(8,128)(2,1)S(1)}, f32[2,2,2,4,3,24,128]{6,5,4,3,2,1,0:T(8,128)S(1)}) custom-call(bf16[24,2,224,256]{3,2,1,0:T(8,128)(2,1)} %bitcast.4, bf16[48,64,112]{2,1,0:T(8,128)(2,1)} %bitcast.5, bf16[3,3,256,128]{3,2,1,0:T(8,128)(2,1)} %kernel.1), custom_call_target="tpu_custom_call" | custom-call | tf_op jit(solution)/shard_map/grads/pallas_call | solution.py:535
  42.7 3.0 %finish.1 = (bf16[24,2,224,256]{3,2,1,0:T(8,128)(2,1)}, f32[2304,128]{1,0:T(8,128)}) custom-call(bf16[24,224,256]{2,1,0:T(8,128)(2,1)S(1)} %get-tuple-element.6.rows, f32[2,2,2,4,3,24,128]{6,5,4,3,2,1,0:T(8,128)S(1)} %get-tuple-element.7.kg_in), custom_call_target="tpu_custom_call" | custom-call | tf_op jit(solution)/shard_map/finish/pallas_call | solution.py:568

commit v3 on v2

--- a/solution.py
+++ b/solution.py
@@ -15,6 +15,7 @@
 BF16 = jnp.bfloat16
 AXES = ("lon", "lat", "chan")
 VMEM_BYTES = 67043328
+EARLY_CUTS = 1
 
 
 def one_hot(shape, test):
@@ -149,13 +150,21 @@
         at = pl.ds(pl.multiple_of(i * LANES, LANES), LANES)
         for s in range(3):
             ev[s, at, :] = picked[s * LANES:(s + 1) * LANES].astype(BF16)
-        edge_out[0, pl.ds(i, 1), :] = picked[LANES + w - 1:LANES + w]
-        edge_out[1, pl.ds(i, 1), :] = picked[LANES:LANES + 1]
         return 0
+
+    def take_edges(rows):
+        for i in rows:
+            edge_out[1, pl.ds(i, 1), :] = fbuf[i, pl.ds(0, PACK), :].astype(F32)[0:1]
+            edge_out[0, pl.ds(i, 1), :] = fbuf[i, pl.ds(2 * w - PACK, PACK), :].astype(F32)[PACK - 2:PACK - 1]
+
+    def take_evens(cuts):
+        for k in cuts:
+            lax.fori_loop(k * step, (k + 1) * step, take_even, 0, unroll=2 - step % 2)
 
     for k in range(plan.fine_cuts):
         fine_in[k].wait()
-        lax.fori_loop(k * step, (k + 1) * step, take_even, 0)
+        take_edges(range(k * step, (k + 1) * step))
+    take_evens(range(EARLY_CUTS))
 
     pad = jnp.zeros((width, LANES - w), BF16) if w < LANES else None
 
@@ -167,11 +176,6 @@
             if pad is not None:
                 block = jnp.concatenate([block, pad[:size]], axis=1)
             xs[at, pl.ds(i * LANES, LANES)] = block
-
-    own_in.wait()
-    if chan_n > 2:
-        pl.when(inner)(lambda: own_extra.wait())
-    fill(0, 0, width, range(1, h + 1))
 
     pl.semaphore_wait(barrier, greeted)
 
@@ -381,22 +385,20 @@
 
     def patch(buffer, base, row, value):
         start = base + row // PACK * PACK
-        at = pl.ds(pl.multiple_of(start, PACK), PACK)
+        at = pl.ds(start, PACK)
         old = buffer[at, :].astype(F32)
         rows = lax.broadcasted_iota(jnp.int32, old.shape, 0)
         buffer[at, :] = jnp.where(rows == row % PACK, value, old).astype(BF16)
 
-    def patch_even(i, _):
+    def patch_even(i):
         base = i * LANES
         patch(ev.at[0], base, 0, edge_in[0, pl.ds(i, 1), :])
         patch(ev.at[2], base, w - 1, edge_in[1, pl.ds(i, 1), :])
-        return 0
-
-    def patch_taps(i, _):
+
+    def patch_taps(i):
         base = i * w
         patch(tt.at[2], base, 0, tedge_in[0, pl.ds(i, 1), :])
         patch(tt.at[0], base, w - 1, tedge_in[1, pl.ds(i, 1), :])
-        return 0
 
     ig_rows = math.gcd(h, 4)
     spread = one_hot((2 * w, w), lambda row, col: row == 2 * col)
@@ -424,8 +426,12 @@
             lax.fori_loop(state["ig"], end, even_grads, 0)
         state["ig"] = end
 
+    take_evens(range(EARLY_CUTS, plan.fine_cuts))
+    own_in.wait()
+    if chan_n > 2:
+        pl.when(inner)(lambda: own_extra.wait())
     halo_arrive(0)
-    fill(0, 0, width, (0, h + 1))
+    fill(0, 0, width, range(h + 2))
     parcels = {}
 
     def begin(d, first, count, s0, s_n):
@@ -438,7 +444,8 @@
     a1 = begin(0, 0, units, 1, 1)
     for n, ref in zip(edge_n, (edge_in.at[0], edge_in.at[1])):
         arrive(ref, n)
-    lax.fori_loop(0, h, patch_even, 0)
+    for i in range(h):
+        patch_even(i)
     parcels[a1] = lat_add(a1, parcels[a1])
     a0 = begin(0, 0, units, 0, 1)
     a2 = begin(0, 0, units, 2, 1)
@@ -453,26 +460,27 @@
             parcel = begin(d, u, 1, 0, 3)
             early.append(parcel)
             parcels[parcel] = lat_add(parcel, parcels[parcel])
-    for parcel in own + [q for q in early if q[0] < last]:
+    finals = [q for q in early if q[0] == last]
+    for parcel in own + early[:-len(finals)]:
         lon_add(parcel, parcels[parcel])
     make_taps()
     tedge_n = [
         send(None, tedge_out.at[0], tedge_in.at[0], {"lon": other("lon", 1)}),
         send(None, tedge_out.at[1], tedge_in.at[1], {"lon": other("lon", -1)}),
     ]
-    finals = [q for q in early if q[0] == last]
     for copy in kernel_in:
         copy.wait()
+    for parcel in finals:
+        finish(parcel, parcels[parcel])
     for n, ref in zip(tedge_n, (tedge_in.at[0], tedge_in.at[1])):
         arrive(ref, n)
-    lax.fori_loop(0, h + 2, patch_taps, 0)
-    for k, parcel in enumerate(finals):
-        finish(parcel, parcels[parcel])
-        some_even_grads(blocks // (2 * len(finals)))
-    for k, parcel in enumerate(finals):
+    for i in range(h + 2):
+        patch_taps(i)
+    for parcel in finals[:-1]:
         relay(parcel[1])
-        some_even_grads(-(-blocks // (2 * len(finals))))
-    some_even_grads(blocks)
+    some_even_grads(3)
+    relay(finals[-1][1])
+    some_even_grads(9)
     for parcel in finals:
         collect(parcel[1])
     for n, dl, block, u in lat_n_of.values():

time: 45.9 us -> 42.3 us (0.922)
  Pallas kernels: 45.1 us -> 41.5 us
    pallas_call x1, Pallas kernels: 42 us -> 38.5 us  [on_device(): pl.pallas_call(functools.partial(grads_kernel, plan, scale), out_shape=(p...]
where the time goes in v3:
time: 42.3 us; the launch traced here: 42.2 us
  Pallas kernels  41.5 us (98%)
  between operations  0.64 us (2%)
    pallas_call x1, Pallas kernels, on_device(): pl.pallas_call(functools.partial(grads_kernel, plan, scale), out_shape=(p...  38.5 us
    pallas_call x1, Pallas kernels, on_device(): pl.pallas_call(functools.partial(finish_kernel, plan), out_shape=(jax.Sha...  3.05 us

profile of v3, /device:TPU:0, one launch (start us, length us, event | category | flops | bytes accessed | tf_op | source)
XLA Modules:
  0.0 42.2 jit_solution(14239042315002836148)
XLA Ops:
  0.6 38.5 %grads.1 = (bf16[24,224,256]{2,1,0:T(8,128)(2,1)S(1)}, f32[2,2,2,4,3,24,128]{6,5,4,3,2,1,0:T(8,128)S(1)}) custom-call(bf16[24,2,224,256]{3,2,1,0:T(8,128)(2,1)} %bitcast.4, bf16[48,64,112]{2,1,0:T(8,128)(2,1)} %bitcast.5, bf16[3,3,256,128]{3,2,1,0:T(8,128)(2,1)} %kernel.1), custom_call_target="tpu_custom_call" | custom-call | tf_op jit(solution)/shard_map/grads/pallas_call | solution.py:543
  39.1 3.0 %finish.1 = (bf16[24,2,224,256]{3,2,1,0:T(8,128)(2,1)}, f32[2304,128]{1,0:T(8,128)}) custom-call(bf16[24,224,256]{2,1,0:T(8,128)(2,1)S(1)} %get-tuple-element.6.rows, f32[2,2,2,4,3,24,128]{6,5,4,3,2,1,0:T(8,128)S(1)} %get-tuple-element.7.kg_in), custom_call_target="tpu_custom_call" | custom-call | tf_op jit(solution)/shard_map/finish/pallas_call | solution.py:576

commit v4 on v3

--- a/solution.py
+++ b/solution.py
@@ -15,7 +15,7 @@
 BF16 = jnp.bfloat16
 AXES = ("lon", "lat", "chan")
 VMEM_BYTES = 67043328
-EARLY_CUTS = 1
+EARLY_CUTS = 2
 
 
 def one_hot(shape, test):
@@ -400,21 +400,43 @@
         patch(tt.at[2], base, 0, tedge_in[0, pl.ds(i, 1), :])
         patch(tt.at[0], base, w - 1, tedge_in[1, pl.ds(i, 1), :])
 
-    ig_rows = math.gcd(h, 4)
+    ig_rows, rim_rows = math.gcd(h, 4), math.gcd(h, 8)
+    rim = (0, w - PACK)
+    middle = ((PACK, w - 2 * PACK),)
     spread = one_hot((2 * w, w), lambda row, col: row == 2 * col)
 
+    def products(first, count, spans):
+        columns = []
+        for r in range(3):
+            for s in range(3):
+                stack = []
+                for k in range(count):
+                    for start, size in spans:
+                        at = pl.multiple_of((first + k + 2 - r) * w + start, PACK)
+                        stack.append(tt[s, pl.ds(at, size), :])
+                columns.append(jnp.concatenate(stack, axis=0))
+        return lax.dot_general(
+            jnp.concatenate(columns, axis=1), kcat[...], (((1,), (1,)), ((), ())), preferred_element_type=F32
+        ).astype(BF16)
+
+    def put(total, first, count, spans):
+        size = sum(n for _, n in spans)
+        for k in range(count):
+            row = jnp.dot(
+                spread[:2 * size, :size], total[k * size:(k + 1) * size], preferred_element_type=F32
+            ).astype(BF16)
+            taken = 0
+            for start, n in spans:
+                rows_out[first + k, pl.ds(2 * start, 2 * n), :] = row[2 * taken:2 * (taken + n)]
+                taken += n
+
     def even_grads(b, _):
-        pieces = []
-        for r in range(3):
-            at = pl.ds(pl.multiple_of((b * ig_rows + 2 - r) * w, PACK), ig_rows * w)
-            for s in range(3):
-                pieces.append(tt[s, at, :])
-        total = lax.dot_general(
-            jnp.concatenate(pieces, axis=1), kcat[...], (((1,), (1,)), ((), ())), preferred_element_type=F32
-        ).astype(BF16)
-        for k in range(ig_rows):
-            row = jnp.dot(spread, total[k * w:(k + 1) * w], preferred_element_type=F32)
-            rows_out[b * ig_rows + k] = row.astype(BF16)
+        put(products(b * ig_rows, ig_rows, middle), b * ig_rows, ig_rows, middle)
+        return 0
+
+    def rim_grads(b, _):
+        spans = tuple((start, PACK) for start in rim)
+        put(products(b * rim_rows, rim_rows, spans), b * rim_rows, rim_rows, spans)
         return 0
 
     blocks = h // ig_rows
@@ -442,11 +464,11 @@
         return parcel
 
     a1 = begin(0, 0, units, 1, 1)
+    parcels[a1] = lat_add(a1, parcels[a1])
     for n, ref in zip(edge_n, (edge_in.at[0], edge_in.at[1])):
         arrive(ref, n)
     for i in range(h):
         patch_even(i)
-    parcels[a1] = lat_add(a1, parcels[a1])
     a0 = begin(0, 0, units, 0, 1)
     a2 = begin(0, 0, units, 2, 1)
     parcels[a0] = lat_add(a0, parcels[a0])
@@ -470,17 +492,20 @@
     ]
     for copy in kernel_in:
         copy.wait()
-    for parcel in finals:
+    some_even_grads(6)
+    for parcel in finals[:-1]:
         finish(parcel, parcels[parcel])
+    some_even_grads(0)
+    finish(finals[-1], parcels[finals[-1]])
+    some_even_grads(blocks)
     for n, ref in zip(tedge_n, (tedge_in.at[0], tedge_in.at[1])):
         arrive(ref, n)
     for i in range(h + 2):
         patch_taps(i)
+    lax.fori_loop(0, h // rim_rows, rim_grads, 0)
     for parcel in finals[:-1]:
         relay(parcel[1])
-    some_even_grads(3)
     relay(finals[-1][1])
-    some_even_grads(9)
     for parcel in finals:
         collect(parcel[1])
     for n, dl, block, u in lat_n_of.values():

time: 42.3 us -> 41.4 us (0.979)
  Pallas kernels: 41.5 us -> 40.6 us
    pallas_call x1, Pallas kernels: 38.5 us -> 37.6 us  [on_device(): pl.pallas_call(functools.partial(grads_kernel, plan, scale), out_shape=(p...]
where the time goes in v4:
time: 41.4 us; the launch traced here: 41.2 us
  Pallas kernels  40.6 us (98%)
  between operations  0.64 us (2%)
    pallas_call x1, Pallas kernels, on_device(): pl.pallas_call(functools.partial(grads_kernel, plan, scale), out_shape=(p...  37.6 us
    pallas_call x1, Pallas kernels, on_device(): pl.pallas_call(functools.partial(finish_kernel, plan), out_shape=(jax.Sha...  3.05 us

profile of v4, /device:TPU:0, one launch (start us, length us, event | category | flops | bytes accessed | tf_op | source)
XLA Modules:
  0.0 41.2 jit_solution(13398808179565971766)
XLA Ops:
  0.6 37.6 %grads.1 = (bf16[24,224,256]{2,1,0:T(8,128)(2,1)S(1)}, f32[2,2,2,4,3,24,128]{6,5,4,3,2,1,0:T(8,128)S(1)}) custom-call(bf16[24,2,224,256]{3,2,1,0:T(8,128)(2,1)} %bitcast.4, bf16[48,64,112]{2,1,0:T(8,128)(2,1)} %bitcast.5, bf16[3,3,256,128]{3,2,1,0:T(8,128)(2,1)} %kernel.1), custom_call_target="tpu_custom_call" | custom-call | tf_op jit(solution)/shard_map/grads/pallas_call | solution.py:568
  38.2 3.0 %finish.1 = (bf16[24,2,224,256]{3,2,1,0:T(8,128)(2,1)}, f32[2304,128]{1,0:T(8,128)}) custom-call(bf16[24,224,256]{2,1,0:T(8,128)(2,1)S(1)} %get-tuple-element.6.rows, f32[2,2,2,4,3,24,128]{6,5,4,3,2,1,0:T(8,128)S(1)} %get-tuple-element.7.kg_in), custom_call_target="tpu_custom_call" | custom-call | tf_op jit(solution)/shard_map/finish/pallas_call | solution.py:601
